TPU v7x, 32 devices: a whole 2x2x4 slice. The times are simulated.
32 devices in a mesh: dp: 16 (over z, y, core), shard: 2 (over x).
Axes of the slice: x: 2, y: 2, z: 4, core: 2. Of those that a mesh axis runs over, the one named last changes fastest.
Arguments:
- tokens: float32 [16384, 1024], P(('dp', 'shard')), may hold values from -6 to 6
- out_grad: float32 [16384, 1024], P(('dp', 'shard')), may hold values from -30 to 30
- segment_ids: int32 [16, 1024], P('dp'), may hold values from 0 to 3, never falling along the last dimension, each value on 1 to 512 neighbouring positions
- qkv_weight: float32 [1024, 3072], P('dp', 'shard'), may hold values from -0.1875 to 0.1875
- proj_weight: float32 [1024, 1024], P('dp', 'shard'), may hold values from -1.5 to 1.5
- up_weight: float32 [1024, 4096], P('dp', 'shard'), may hold values from -0.1875 to 0.1875
- down_weight: float32 [4096, 1024], P('dp', 'shard'), may hold values from -0.09375 to 0.09375
- vectors: float32 [12, 1024], P(None, ('dp', 'shard')), may hold values from -4 to 4
- qkv_moments: float32 [2, 1024, 3072], P(None, 'dp', 'shard'), may hold values from -0.05 to 0.05
- proj_moments: float32 [2, 1024, 1024], P(None, 'dp', 'shard'), may hold values from -0.05 to 0.05
- up_moments: float32 [2, 1024, 4096], P(None, 'dp', 'shard'), may hold values from -0.05 to 0.05
- down_moments: float32 [2, 4096, 1024], P(None, 'dp', 'shard'), may hold values from -0.05 to 0.05
- vector_moments: float32 [2, 12, 1024], P(None, None, ('dp', 'shard')), may hold values from -1 to 1
Outputs:
- block_out: float32 [16384, 1024], P(('dp', 'shard'))
- tokens_grad: float32 [16384, 1024], P(('dp', 'shard'))
- qkv_grad: float32 [1024, 3072], P('dp', 'shard')
- proj_grad: float32 [1024, 1024], P('dp', 'shard')
- up_grad: float32 [1024, 4096], P('dp', 'shard')
- down_grad: float32 [4096, 1024], P('dp', 'shard')
- vectors_grad: float32 [12, 1024], P(None, ('dp', 'shard'))
- qkv_new: float32 [1024, 3072], P('dp', 'shard')
- proj_new: float32 [1024, 1024], P('dp', 'shard')
- up_new: float32 [1024, 4096], P('dp', 'shard')
- down_new: float32 [4096, 1024], P('dp', 'shard')
- vectors_new: float32 [12, 1024], P(None, ('dp', 'shard'))
- qkv_moments_new: float32 [2, 1024, 3072], P(None, 'dp', 'shard')
- proj_moments_new: float32 [2, 1024, 1024], P(None, 'dp', 'shard')
- up_moments_new: float32 [2, 1024, 4096], P(None, 'dp', 'shard')
- down_moments_new: float32 [2, 4096, 1024], P(None, 'dp', 'shard')
- vector_moments_new: float32 [2, 12, 1024], P(None, None, ('dp', 'shard'))
All inputs are finite; a program needn't handle non-finite values.
Results may differ from a plain program's by a relative error of at most 0.011.
Values may be sent and summed in bfloat16 or wider, within the bound.
A program may use at most 320 MiB of HBM per device.

v0:
```python
import math
import jax
import jax.numpy as jnp
from jax import lax
from jax.sharding import PartitionSpec as P

D = 1024
FF = 4096
HD = 64
ROT = 16
STEP = 4
VROWS = 12
NPARAM = 12595200
ln_eps = 1e-05
beta_one = 0.9
beta_two = 0.95
learn_rate = 0.005
decay_rate = 0.01
adam_eps = 1e-08
rope_base = 10000.0


def norm_rows(inputs, gain_row, bias_row):
    center = inputs - jnp.mean(inputs, axis=-1, keepdims=True)
    inverse = lax.rsqrt(jnp.mean(center * center, axis=-1, keepdims=True) + ln_eps)
    unit_rows = center * inverse
    return (unit_rows * gain_row + bias_row, unit_rows, inverse)


def norm_back(upstream, unit_rows, inverse, gain_row):
    gain_grad = jnp.sum(upstream * unit_rows, axis=0)
    bias_grad = jnp.sum(upstream, axis=0)
    scaled_up = upstream * gain_row
    mean_plain = jnp.mean(scaled_up, axis=-1, keepdims=True)
    mean_unit = jnp.mean(scaled_up * unit_rows, axis=-1, keepdims=True)
    return (inverse * (scaled_up - mean_plain - unit_rows * mean_unit), gain_grad, bias_grad)


def doc_positions(segment_row):
    length_all = segment_row.shape[0]
    indices = jnp.arange(length_all, dtype=jnp.int32)
    starting = jnp.concatenate(
        [jnp.ones((1,), dtype=jnp.bool_), segment_row[1:] != segment_row[:-1]]
    )
    begins = lax.cummax(jnp.where(starting, indices, 0), axis=0)
    return indices - begins


def rotary_tables(positions, rot_dims):
    half_dims = rot_dims // 2
    exponent = jnp.arange(half_dims, dtype=jnp.float32) * (2.0 / rot_dims)
    inverse_freq = jnp.exp(-math.log(rope_base) * exponent)
    angles = positions.astype(jnp.float32)[:, None] * inverse_freq[None, :]
    return (jnp.cos(angles)[:, None, :], jnp.sin(angles)[:, None, :])


def rotate(head_rows, cosine_table, sine_table):
    half_dims = cosine_table.shape[-1]
    lower_half = head_rows[..., :half_dims]
    upper_half = head_rows[..., half_dims : 2 * half_dims]
    return jnp.concatenate(
        [
            lower_half * cosine_table - upper_half * sine_table,
            upper_half * cosine_table + lower_half * sine_table,
            head_rows[..., 2 * half_dims :],
        ],
        axis=-1,
    )


def gelu_pair(pre_act):
    normal_cdf = 0.5 * (1.0 + lax.erf(pre_act * (1.0 / math.sqrt(2.0))))
    density = jnp.exp(-0.5 * pre_act * pre_act) * (1.0 / math.sqrt(2.0 * math.pi))
    return (pre_act * normal_cdf, normal_cdf + pre_act * density)


def times_transposed(left, right):
    return lax.dot_general(
        left, right, (((1,), (1,)), ((), ())), preferred_element_type=jnp.float32
    )


def transposed_times(left, right):
    return lax.dot_general(
        left, right, (((0,), (0,)), ((), ())), preferred_element_type=jnp.float32
    )


def adam_update(weight, moments, gradient, clip_factor):
    clipped = gradient * clip_factor
    first_new = beta_one * moments[0] + (1.0 - beta_one) * clipped
    second_new = beta_two * moments[1] + (1.0 - beta_two) * clipped * clipped
    fix_first = 1.0 - math.pow(beta_one, STEP)
    fix_second = 1.0 - math.pow(beta_two, STEP)
    direction = first_new / fix_first / (jnp.sqrt(second_new / fix_second) + adam_eps)
    return (
        weight - learn_rate * (direction + decay_rate * weight),
        jnp.stack([first_new, second_new]),
    )


def shards(
    tokens,
    out_grad,
    segment_ids,
    qkv_weight,
    proj_weight,
    up_weight,
    down_weight,
    vectors,
    qkv_moments,
    proj_moments,
    up_moments,
    down_moments,
    vector_moments,
):
    columns_full = (
        lax.all_gather(qkv_weight.astype(jnp.bfloat16), "shard", axis=1, tiled=True),
        lax.all_gather(proj_weight.astype(jnp.bfloat16), "shard", axis=1, tiled=True),
        lax.all_gather(up_weight.astype(jnp.bfloat16), "shard", axis=1, tiled=True),
        lax.all_gather(down_weight.astype(jnp.bfloat16), "shard", axis=1, tiled=True),
        lax.all_gather(vectors.astype(jnp.bfloat16), "shard", axis=1, tiled=True),
    )
    qkv_work, proj_work, up_work, down_work, vec_bf = (
        lax.all_gather(columns_full[0], "dp", axis=0, tiled=True),
        lax.all_gather(columns_full[1], "dp", axis=0, tiled=True),
        lax.all_gather(columns_full[2], "dp", axis=0, tiled=True),
        lax.all_gather(columns_full[3], "dp", axis=0, tiled=True),
        lax.all_gather(columns_full[4], "dp", axis=1, tiled=True),
    )
    vec_work = vec_bf.astype(jnp.float32)
    head_count = D // HD
    score_scale = 1.0 / math.sqrt(HD)
    local_rows = tokens.shape[0]
    segment_row = segment_ids[0]
    length_all = segment_row.shape[0]
    row_start = lax.axis_index("shard") * local_rows
    query_index = row_start + jnp.arange(local_rows, dtype=jnp.int32)
    query_segment = lax.dynamic_slice_in_dim(segment_row, row_start, local_rows)
    positions = lax.dynamic_slice_in_dim(doc_positions(segment_row), row_start, local_rows)
    normed_one, unit_one, inverse_one = norm_rows(tokens, vec_work[0], vec_work[1])
    hidden_one = normed_one.astype(jnp.bfloat16)
    mixed_rows = jnp.dot(hidden_one, qkv_work, preferred_element_type=jnp.float32)
    query_raw = (mixed_rows[:, :D] + vec_work[4]).reshape(local_rows, head_count, HD)
    key_raw = mixed_rows[:, D : 2 * D].reshape(local_rows, head_count, HD)
    value_bf = (mixed_rows[:, 2 * D :] + vec_work[5]).astype(jnp.bfloat16)
    cosine_table, sine_table = rotary_tables(positions, ROT)
    query_bf = rotate(query_raw, cosine_table, sine_table).astype(jnp.bfloat16)
    key_bf = rotate(key_raw, cosine_table, sine_table).astype(jnp.bfloat16).reshape(local_rows, D)
    key_piece = lax.all_gather(key_bf, "shard", axis=0, tiled=True)
    value_piece = lax.all_gather(value_bf, "shard", axis=0, tiled=True)
    piece_rows = key_piece.shape[0]
    key_heads = key_piece.reshape(piece_rows, head_count, HD)
    value_heads = value_piece.reshape(piece_rows, head_count, HD)
    key_index = jnp.arange(piece_rows, dtype=jnp.int32)
    allowed = (segment_row[None, :] == query_segment[:, None]) & (
        key_index[None, :] <= query_index[:, None]
    )
    scores = (
        jnp.einsum("qhd,khd->hqk", query_bf, key_heads, preferred_element_type=jnp.float32)
        * score_scale
    )
    exp_scores = jnp.where(allowed[None], jnp.exp(scores), 0.0)
    numerator = jnp.einsum(
        "hqk,khd->qhd",
        exp_scores.astype(jnp.bfloat16),
        value_heads,
        preferred_element_type=jnp.float32,
    )
    numerator, totals = (numerator, jnp.sum(exp_scores, axis=-1))
    attended = numerator / jnp.transpose(totals)[:, :, None]
    log_totals = jnp.log(totals)
    attended_bf = attended.reshape(local_rows, D).astype(jnp.bfloat16)
    proj_out = jnp.dot(attended_bf, proj_work, preferred_element_type=jnp.float32) + vec_work[6]
    normed_two, unit_two, inverse_two = norm_rows(tokens, vec_work[2], vec_work[3])
    hidden_two = normed_two.astype(jnp.bfloat16)
    pre_act = jnp.dot(hidden_two, up_work, preferred_element_type=jnp.float32) + vec_work[
        8:
    ].reshape(FF)
    act_values, act_slope = gelu_pair(pre_act)
    act_bf = act_values.astype(jnp.bfloat16)
    block_out = (
        tokens
        + proj_out
        + (jnp.dot(act_bf, down_work, preferred_element_type=jnp.float32) + vec_work[7])
    )
    cot_bf = out_grad.astype(jnp.bfloat16)
    down_part = transposed_times(act_bf, cot_bf)
    proj_part = transposed_times(attended_bf, cot_bf)
    cot_sum = jnp.sum(out_grad, axis=0)
    grad_pre = times_transposed(cot_bf, down_work) * act_slope
    grad_pre_bf = grad_pre.astype(jnp.bfloat16)
    up_part = transposed_times(hidden_two, grad_pre_bf)
    rows_two, ln2_gain_part, ln2_bias_part = norm_back(
        times_transposed(grad_pre_bf, up_work), unit_two, inverse_two, vec_work[2]
    )
    grad_att_bf = (
        times_transposed(cot_bf, proj_work).astype(jnp.bfloat16).reshape(local_rows, head_count, HD)
    )
    keys_all, values_all = (
        lax.all_gather(key_bf, "shard", axis=0, tiled=True),
        lax.all_gather(value_bf, "shard", axis=0, tiled=True),
    )
    key_heads = keys_all.reshape(length_all, head_count, HD)
    value_heads = values_all.reshape(length_all, head_count, HD)
    key_index = jnp.arange(length_all, dtype=jnp.int32)
    allowed = (segment_row[None, :] == query_segment[:, None]) & (
        key_index[None, :] <= query_index[:, None]
    )
    scores = (
        jnp.einsum("qhd,khd->hqk", query_bf, key_heads, preferred_element_type=jnp.float32)
        * score_scale
    )
    probability = jnp.where(allowed[None], jnp.exp(scores - log_totals[:, :, None]), 0.0)
    grad_prob = jnp.einsum(
        "qhd,khd->hqk", grad_att_bf, value_heads, preferred_element_type=jnp.float32
    )
    row_delta = jnp.transpose(jnp.sum(grad_att_bf.astype(jnp.float32) * attended, axis=-1))
    grad_score = (probability * (grad_prob - row_delta[:, :, None]) * score_scale).astype(
        jnp.bfloat16
    )
    grad_query = jnp.einsum(
        "hqk,khd->qhd", grad_score, key_heads, preferred_element_type=jnp.float32
    )
    grad_query = rotate(grad_query, cosine_table, -sine_table).reshape(local_rows, D)
    key_terms = jnp.einsum(
        "hqk,qhd->khd", grad_score, query_bf, preferred_element_type=jnp.float32
    ).reshape(length_all, D)
    value_terms = jnp.einsum(
        "hqk,qhd->khd",
        probability.astype(jnp.bfloat16),
        grad_att_bf,
        preferred_element_type=jnp.float32,
    ).reshape(length_all, D)
    key_value_grad = lax.psum_scatter(
        jnp.concatenate([key_terms, value_terms], axis=1), "shard", scatter_dimension=0, tiled=True
    )
    grad_key = rotate(
        key_value_grad[:, :D].reshape(local_rows, head_count, HD), cosine_table, -sine_table
    ).reshape(local_rows, D)
    grad_value = key_value_grad[:, D:]
    grad_mixed_bf = jnp.concatenate([grad_query, grad_key, grad_value], axis=1).astype(jnp.bfloat16)
    qkv_part = transposed_times(hidden_one, grad_mixed_bf)
    rows_one, ln1_gain_part, ln1_bias_part = norm_back(
        times_transposed(grad_mixed_bf, qkv_work), unit_one, inverse_one, vec_work[0]
    )
    tokens_grad = out_grad + rows_one + rows_two
    vec_part = jnp.concatenate(
        [
            jnp.stack(
                [
                    ln1_gain_part,
                    ln1_bias_part,
                    ln2_gain_part,
                    ln2_bias_part,
                    jnp.sum(grad_query, axis=0),
                    jnp.sum(grad_value, axis=0),
                    cot_sum,
                    cot_sum,
                ]
            ),
            jnp.sum(grad_pre, axis=0).reshape(FF // D, D),
        ],
        axis=0,
    )
    groups = lax.axis_size("dp")
    members = lax.axis_size("shard")
    owners = groups * members
    vec_split = vec_part.reshape(VROWS, groups, members, D // owners)
    group_sums = (
        lax.psum_scatter(qkv_part, "shard", scatter_dimension=1, tiled=True),
        lax.psum_scatter(proj_part, "shard", scatter_dimension=1, tiled=True),
        lax.psum_scatter(up_part, "shard", scatter_dimension=1, tiled=True),
        lax.psum_scatter(down_part, "shard", scatter_dimension=1, tiled=True),
        lax.psum_scatter(vec_split, "shard", scatter_dimension=2, tiled=True),
    )
    owner_sums = (
        lax.psum_scatter(group_sums[0], "dp", scatter_dimension=0, tiled=True),
        lax.psum_scatter(group_sums[1], "dp", scatter_dimension=0, tiled=True),
        lax.psum_scatter(group_sums[2], "dp", scatter_dimension=0, tiled=True),
        lax.psum_scatter(group_sums[3], "dp", scatter_dimension=0, tiled=True),
        lax.psum_scatter(group_sums[4], "dp", scatter_dimension=1, tiled=True),
    )
    qkv_grad = owner_sums[0]
    proj_grad = owner_sums[1]
    up_grad = owner_sums[2]
    down_grad = owner_sums[3]
    vectors_grad = owner_sums[4].reshape(VROWS, D // owners)
    local_square = (
        jnp.sum(qkv_grad * qkv_grad)
        + jnp.sum(proj_grad * proj_grad)
        + jnp.sum(up_grad * up_grad)
        + jnp.sum(down_grad * down_grad)
        + jnp.sum(vectors_grad * vectors_grad)
    )
    square_total = lax.psum(local_square, ("dp", "shard"))
    norm_limit = math.sqrt(NPARAM)
    clip_factor = norm_limit / jnp.maximum(jnp.sqrt(square_total), norm_limit)
    qkv_new, qkv_moments_new = adam_update(qkv_weight, qkv_moments, qkv_grad, clip_factor)
    proj_new, proj_moments_new = adam_update(proj_weight, proj_moments, proj_grad, clip_factor)
    up_new, up_moments_new = adam_update(up_weight, up_moments, up_grad, clip_factor)
    down_new, down_moments_new = adam_update(down_weight, down_moments, down_grad, clip_factor)
    vectors_new, vector_moments_new = adam_update(
        vectors, vector_moments, vectors_grad, clip_factor
    )
    return (
        block_out,
        tokens_grad,
        qkv_grad,
        proj_grad,
        up_grad,
        down_grad,
        vectors_grad,
        qkv_new,
        proj_new,
        up_new,
        down_new,
        vectors_new,
        qkv_moments_new,
        proj_moments_new,
        up_moments_new,
        down_moments_new,
        vector_moments_new,
    )


def solution(mesh):
    placed = (
        P(("dp", "shard"), None),
        P(("dp", "shard"), None),
        P("dp", None),
        P("dp", "shard"),
        P("dp", "shard"),
        P("dp", "shard"),
        P("dp", "shard"),
        P(None, ("dp", "shard")),
        P(None, "dp", "shard"),
        P(None, "dp", "shard"),
        P(None, "dp", "shard"),
        P(None, "dp", "shard"),
        P(None, None, ("dp", "shard")),
    )
    return jax.shard_map(
        shards,
        mesh=mesh,
        in_specs=placed,
        out_specs=(
            P(("dp", "shard"), None),
            P(("dp", "shard"), None),
            P("dp", "shard"),
            P("dp", "shard"),
            P("dp", "shard"),
            P("dp", "shard"),
            P(None, ("dp", "shard")),
            P("dp", "shard"),
            P("dp", "shard"),
            P("dp", "shard"),
            P("dp", "shard"),
            P(None, ("dp", "shard")),
            P(None, "dp", "shard"),
            P(None, "dp", "shard"),
            P(None, "dp", "shard"),
            P(None, "dp", "shard"),
            P(None, None, ("dp", "shard")),
        ),
        check_vma=False,
    )
```

profile of v0, /device:TPU:0, one launch (start us, length us, event | category | flops | bytes accessed | tf_op | source)
XLA Modules:
  0.0 1481.1 jit_solution(18126317219042445174)
XLA Ops:
  8.4 8.6 all_gather.40
  27.7 22.3 %all-gather.1 = bf16[16,64,12]{1,2,0:T(8,128)(2,1)S(1)} all-gather(bf16[1,64,12]{1,2,0:T(8,128)(2,1)S(1)} %reshape.337), channel_id=1, replica_groups=mesh['dp'=16,'shard'=2] {'dp'}, dimensions={0}, use_global_device_ids=true | all-gather | bytes 26112 | tf_op jit(solution)/shard_map/all_gather | solution.py:129
  52.8 27.5 %all-gather.9.cloned.1.call-done = bf16[1024,3072]{1,0:T(8,128)(2,1)} async-done(((bf16[64,3072]{1,0:T(8,128)(2,1)}), bf16[1024,3072]{1,0:T(8,128)(2,1)}) %all-gather.9.cloned.1.call-update) | async-done | bytes 6291472 | tf_op jit(solution)/shard_map/all_gather | solution.py:125
  98.4 9.4 all_gather.46
  128.6 28.0 %all-gather.13.cloned.1.call-done = bf16[1024,1024]{0,1:T(8,128)(2,1)} async-done(((bf16[512,1024]{0,1:T(8,128)(2,1)}), bf16[1024,1024]{0,1:T(8,128)(2,1)}) %all-gather.13.cloned.1.call-update) | async-done | bytes 2097168 | tf_op jit(solution)/shard_map/all_gather | solution.py:150
  156.6 17.5 %fusion = (f32[16,512]{1,0:T(8,128)S(1)}, f32[16,512,1024]{2,1,0:T(8,128)}) fusion(pred[512,1024]{1,0:T(8,128)(4,1)S(1)} %copy-done.22, bf16[1024,16,64]{0,2,1:T(8,128)(2,1)} %bitcast.176, bf16[512,16,48]{0,2,1:T(8,128)(2,1)S(1)} %slice.267, bf16[512,16,8]{0,2,1:T(8,128)(2,1)S(1)} %copy-done.23, bf16[512,16,8]{0,2,1:T(8,128)(2,1)S(1)} %get-tuple-element.73), kind=kOutput, calls=%fused_computation.3 | convolution fusion | flops 1102045184 | bytes 37257216 | tf_op jit(solution)/shard_map/qhd,khd->hqk/dot_general | solution.py:160
  174.2 17.6 %all-gather.11.cloned.1.call-done = bf16[1024,1024]{1,0:T(8,128)(2,1)} async-done(((bf16[512,1024]{1,0:T(8,128)(2,1)}), bf16[1024,1024]{1,0:T(8,128)(2,1)}) %all-gather.11.cloned.1.call-update) | async-done | bytes 2097168 | tf_op jit(solution)/shard_map/all_gather | solution.py:151
  194.6 15.7 %multiply_reduce_fusion.4 = (f32[512,16]{0,1:T(8,128)S(1)}, bf16[512,16,64]{0,2,1:T(8,128)(2,1)}) fusion(bf16[512,1024]{0,1:T(8,128)(2,1)} %copy.71, f32[512,16]{0,1:T(8,128)S(1)} %bitcast.190, bf16[1024,16,64]{0,2,1:T(8,128)(2,1)S(1)} %bitcast.178, f32[16,512,1024]{2,1,0:T(8,128)} %get-tuple-element.113, pred[512,1024]{1,0:T(8,128)(4,1)} %fusion.19), kind=kOutput, calls=%fused_computation.34 | convolution fusion | flops 1101520896 | bytes 38338560 | tf_op jit(solution)/shard_map/hqk,khd->qhd/dot_general | solution.py:164
  210.3 22.3 %multiply_convert_fusion = bf16[16,512,1024]{2,1,0:T(8,128)(2,1)} fusion(f32[16,512,1024]{2,1,0:T(8,128)} %get-tuple-element.113, f32[16,512]{1,0:T(8,128)S(1)} %bitcast.212, f32[16,512]{1,0:T(8,128)S(1)} %log.7, pred[512,1024]{1,0:T(8,128)(4,1)} %fusion.19, bf16[512,16,64]{0,2,1:T(8,128)(2,1)} %bitcast.184, bf16[1024,16,64]{0,2,1:T(8,128)(2,1)S(1)} %bitcast.179), kind=kOutput, calls=%fused_computation | convolution fusion | flops 1132462080 | bytes 54067200 | tf_op jit(solution)/shard_map/qhd,khd->hqk/dot_general | solution.py:215
  232.7 9.0 fusion.28
  241.7 16.6 %fusion.5 = f32[16,64,1024]{2,1,0:T(8,128)} fusion(bf16[512,16,64]{0,2,1:T(8,128)(2,1)} %bitcast.185, f32[16,512,1024]{2,1,0:T(8,128)} %get-tuple-element.113, f32[16,512]{1,0:T(8,128)} %copy-done.31, pred[512,1024]{1,0:T(8,128)(4,1)} %fusion.19), kind=kOutput, calls=%fused_computation.7 | convolution fusion | flops 1107296256 | bytes 39354368 | tf_op jit(solution)/shard_map/hqk,qhd->khd/dot_general | solution.py:229
  271.6 10.7 multiply_convert_fusion.1
  282.3 60.7 %all-gather.19.cloned.1.call-done = bf16[4096,1024]{1,0:T(8,128)(2,1)} async-done(((bf16[256,1024]{1,0:T(8,128)(2,1)}), bf16[4096,1024]{1,0:T(8,128)(2,1)}) %all-gather.19.cloned.1.call-update) | async-done | bytes 8388624 | tf_op jit(solution)/shard_map/all_gather | solution.py:128
  343.0 10.7 fusion.68
  355.7 8.4 fusion.15
  364.1 10.6 fusion.71
  375.0 13.2 convolution_bitcast_fusion
  390.9 52.3 %reduce-scatter.12.cloned.1.call-done = f32[512,2048]{0,1:T(8,128)} async-done(((f32[1024,2048]{0,1:T(8,128)}), f32[512,2048]{0,1:T(8,128)}) %reduce-scatter.12.cloned.1.call-update) | async-done | bytes 4194320 | tf_op jit(solution)/shard_map/reduce_scatter | solution.py:235
  450.9 9.6 fusion.24
  461.4 38.5 %reduce-scatter.18.cloned.1.call-done = f32[1024,512]{1,0:T(8,128)} async-done(((f32[1024,1024]{1,0:T(8,128)}), f32[1024,512]{1,0:T(8,128)}) %reduce-scatter.18.cloned.1.call-update) | async-done | bytes 2097168 | tf_op jit(solution)/shard_map/reduce_scatter | solution.py:272
  500.2 8.6 fusion.25
  509.2 11.7 multiply_reduce_fusion
  522.2 169.3 %reduce-scatter.22.cloned.1.call-done = f32[1024,2048]{1,0:T(8,128)} async-done(((f32[1024,4096]{1,0:T(8,128)}), f32[1024,2048]{1,0:T(8,128)}) %reduce-scatter.22.cloned.1.call-update) | async-done | bytes 8388624 | tf_op jit(solution)/shard_map/reduce_scatter | solution.py:273
  691.6 191.3 %reduce-scatter.26.cloned.1.call-done = f32[4096,512]{1,0:T(8,128)} async-done(((f32[4096,1024]{1,0:T(8,128)}), f32[4096,512]{1,0:T(8,128)}) %reduce-scatter.26.cloned.1.call-update) | async-done | bytes 8388624 | tf_op jit(solution)/shard_map/reduce_scatter | solution.py:274
  883.0 146.8 %reduce-scatter.14.cloned.1.call-done = f32[1024,1536]{1,0:T(8,128)} async-done(((f32[1024,3072]{1,0:T(8,128)}), f32[1024,1536]{1,0:T(8,128)}) %reduce-scatter.14.cloned.1.call-update) | async-done | bytes 6291472 | tf_op jit(solution)/shard_map/reduce_scatter | solution.py:271
  1042.0 53.7 %reduce-scatter.20.cloned.1.call-done = f32[64,512]{1,0:T(8,128)} async-done(((f32[1024,512]{1,0:T(8,128)}), f32[64,512]{1,0:T(8,128)}) %reduce-scatter.20.cloned.1.call-update) | async-done | bytes 131088 | tf_op jit(solution)/shard_map/reduce_scatter | solution.py:279
  1097.3 11.3 reduce-scatter.30.cloned.1.call-done
  1108.6 65.1 %all-reduce = f32[12,16,1,32]{3,2,1,0:T(1,128)S(1)} all-reduce(f32[12,16,1,32]{3,2,1,0:T(1,128)} %bitcast.188), channel_id=12, replica_groups=mesh['dp'=16,'shard'=2] {'dp'}, use_global_device_ids=true, to_apply=%region_28.29.clone | all-reduce | flops 6144 | bytes 49152
  1175.0 42.1 %reduce-scatter.24.cloned.1.call-done = f32[64,2048]{1,0:T(8,128)} async-done(((f32[1024,2048]{1,0:T(8,128)}), f32[64,2048]{1,0:T(8,128)}) %reduce-scatter.24.cloned.1.call-update) | async-done | bytes 524304 | tf_op jit(solution)/shard_map/reduce_scatter | solution.py:280
  1218.9 105.8 %reduce-scatter.28.cloned.1.call-done = f32[256,512]{1,0:T(8,128)} async-done(((f32[4096,512]{1,0:T(8,128)}), f32[256,512]{1,0:T(8,128)}) %reduce-scatter.28.cloned.1.call-update) | async-done | bytes 524304 | tf_op jit(solution)/shard_map/reduce_scatter | solution.py:281
  1326.5 87.3 %reduce-scatter.16.cloned.1.call-done = f32[64,1536]{1,0:T(8,128)} async-done(((f32[1024,1536]{1,0:T(8,128)}), f32[64,1536]{1,0:T(8,128)}) %reduce-scatter.16.cloned.1.call-update) | async-done | bytes 393232 | tf_op jit(solution)/shard_map/reduce_scatter | solution.py:278
  1423.2 39.6 %psum.7 = f32[]{:T(128)} all-reduce(f32[]{:T(128)S(6)} %add.283), channel_id=1, replica_groups=mesh['dp'=16,'shard'=2] {'dp','shard'}, use_global_device_ids=true, to_apply=%region_34.35 | all-reduce | flops 1 | bytes 8 | tf_op jit(solution)/shard_map/psum | solution.py:296
  (229 shorter events, 120.2 us)
Async XLA Ops:
  7.2 16.0 %copy-start.32 = (f32[12,32]{1,0:T(8,128)S(1)}, f32[12,32]{1,0:T(8,128)}, u32[]{:S(2)}) copy-start(f32[12,32]{1,0:T(8,128)} %param.20) | copy-start | bytes 4612
  7.2 42.8 %copy-start.30 = (s32[1,1024]{1,0:T(1,128)S(1)}, s32[1,1024]{1,0:T(1,128)}, u32[]{:S(2)}) copy-start(s32[1,1024]{1,0:T(1,128)} %param.15) | copy-start | bytes 12292
  7.2 43.4 %copy-start = (f32[512,1024]{1,0:T(8,128)S(1)}, f32[512,1024]{1,0:T(8,128)}, u32[]{:S(2)}) copy-start(f32[512,1024]{1,0:T(8,128)} %param.13) | copy-start | bytes 6291460
  7.2 73.1 %all-gather.9.cloned.1.call-start = ((), (), s32[]{:S(2)}) async-start(), calls=%async_computation.10 | async-start | bytes 6684672 | tf_op jit(solution)/shard_map/all_gather | solution.py:125
  17.1 105.6 %all-gather.15.cloned.1.call-start = ((), (), s32[]{:S(2)}) async-start(), calls=%async_computation.13 | async-start | bytes 2228224 | tf_op jit(solution)/shard_map/all_gather | solution.py:126
  23.1 133.5 %all-gather.13.cloned.1.call-start = ((), (), s32[]{:S(2)}) async-start(), calls=%async_computation.12 | async-start | bytes 3145728 | tf_op jit(solution)/shard_map/all_gather | solution.py:150
  52.2 42.4 %copy-start.27 = (f32[512,8]{0,1:T(8,128)}, f32[512,8]{0,1:T(8,128)S(1)}, u32[]{:S(2)}) copy-start(f32[512,8]{0,1:T(8,128)S(1)} %get-tuple-element.111) | copy-start | bytes 49156
  52.8 33.2 %copy-start.35 = (f32[1,1024]{1,0:T(1,128)}, f32[1,1024]{1,0:T(1,128)S(1)}, u32[]{:S(2)}) copy-start(f32[1,1024]{1,0:T(1,128)S(1)} %get-tuple-element.100) | copy-start | bytes 12292
  52.8 33.3 %copy-start.41 = (f32[1,1024]{1,0:T(1,128)}, f32[1,1024]{1,0:T(1,128)S(1)}, u32[]{:S(2)}) copy-start(f32[1,1024]{1,0:T(1,128)S(1)} %get-tuple-element.99) | copy-start | bytes 12292
  97.7 10.2 copy-start.5
  97.7 94.0 %all-gather.11.cloned.1.call-start = ((), (), s32[]{:S(2)}) async-start(), calls=%async_computation.11 | async-start | bytes 3145728 | tf_op jit(solution)/shard_map/all_gather | solution.py:151
  98.3 172.7 %all-gather.17.cloned.1.call-start = ((), (), s32[]{:S(2)}) async-start(), calls=%async_computation.14 | async-start | bytes 8912896 | tf_op jit(solution)/shard_map/all_gather | solution.py:127
  98.4 19.4 %copy-start.4 = (f32[512,1024]{1,0:T(8,128)S(1)}, f32[512,1024]{1,0:T(8,128)}, u32[]{:S(2)}) copy-start(f32[512,1024]{1,0:T(8,128)} %param.14) | copy-start | bytes 6291460
  107.8 235.2 %all-gather.19.cloned.1.call-start = ((), (), s32[]{:S(2)}) async-start(), calls=%async_computation.15 | async-start | bytes 8912896 | tf_op jit(solution)/shard_map/all_gather | solution.py:128
  116.3 326.9 %reduce-scatter.12.cloned.1.call-start = ((), (), s32[]{:S(2)}) async-start(), calls=%async_computation.16 | async-start | bytes 12582912 | tf_op jit(solution)/shard_map/reduce_scatter | solution.py:235
  125.6 31.1 %copy-start.22 = (pred[512,1024]{1,0:T(8,128)(4,1)S(1)}, pred[512,1024]{1,0:T(8,128)(4,1)}, u32[]{:S(2)}) copy-start(pred[512,1024]{1,0:T(8,128)(4,1)} %fusion.19) | copy-start | bytes 1572868
  125.6 31.1 %copy-start.23 = (bf16[512,16,8]{0,2,1:T(8,128)(2,1)S(1)}, bf16[512,16,8]{0,2,1:T(8,128)(2,1)}, u32[]{:S(2)}) copy-start(bf16[512,16,8]{0,2,1:T(8,128)(2,1)} %get-tuple-element.74) | copy-start | bytes 393220
  174.2 36.2 %copy-start.31 = (f32[16,512]{1,0:T(8,128)}, f32[16,512]{1,0:T(8,128)S(1)}, u32[]{:S(2)}) copy-start(f32[16,512]{1,0:T(8,128)S(1)} %log.7) | copy-start | bytes 98308
  210.3 22.3 %copy-start.24 = (bf16[512,16,8]{0,2,1:T(8,128)(2,1)S(1)}, bf16[512,16,8]{0,2,1:T(8,128)(2,1)}, u32[]{:S(2)}) copy-start(bf16[512,16,8]{0,2,1:T(8,128)(2,1)} %get-tuple-element.74) | copy-start | bytes 393220
  265.1 234.8 %reduce-scatter.18.cloned.1.call-start = ((), (), s32[]{:S(2)}) async-start(), calls=%async_computation.19 | async-start | bytes 6291456 | tf_op jit(solution)/shard_map/reduce_scatter | solution.py:272
  270.0 421.5 %reduce-scatter.22.cloned.1.call-start = ((), (), s32[]{:S(2)}) async-start(), calls=%async_computation.21 | async-start | bytes 25165824 | tf_op jit(solution)/shard_map/reduce_scatter | solution.py:273
  364.1 518.8 %reduce-scatter.26.cloned.1.call-start = ((), (), s32[]{:S(2)}) async-start(), calls=%async_computation.23 | async-start | bytes 25165824 | tf_op jit(solution)/shard_map/reduce_scatter | solution.py:274
  374.8 655.0 %reduce-scatter.14.cloned.1.call-start = ((), (), s32[]{:S(2)}) async-start(), calls=%async_computation.17 | async-start | bytes 18874368 | tf_op jit(solution)/shard_map/reduce_scatter | solution.py:271
  460.6 635.2 %reduce-scatter.20.cloned.1.call-start = ((), (), s32[]{:S(2)}) async-start(), calls=%async_computation.20 | async-start | bytes 2228224 | tf_op jit(solution)/shard_map/reduce_scatter | solution.py:279
  500.0 608.7 %reduce-scatter.30.cloned.1.call-start = ((), (), s32[]{:S(2)}) async-start(), calls=%async_computation.25 | async-start | bytes 294912 | tf_op jit(solution)/shard_map/reduce_scatter | solution.py:275
  522.1 695.0 %reduce-scatter.24.cloned.1.call-start = ((), (), s32[]{:S(2)}) async-start(), calls=%async_computation.22 | async-start | bytes 8912896 | tf_op jit(solution)/shard_map/reduce_scatter | solution.py:280
  691.5 633.2 %reduce-scatter.28.cloned.1.call-start = ((), (), s32[]{:S(2)}) async-start(), calls=%async_computation.24 | async-start | bytes 8912896 | tf_op jit(solution)/shard_map/reduce_scatter | solution.py:281
  882.9 530.9 %reduce-scatter.16.cloned.1.call-start = ((), (), s32[]{:S(2)}) async-start(), calls=%async_computation.18 | async-start | bytes 6684672 | tf_op jit(solution)/shard_map/reduce_scatter | solution.py:278
  1175.0 289.2 %copy-start.34 = (f32[12,32]{1,0:T(8,128)}, f32[12,32]{1,0:T(8,128)S(1)}, u32[]{:S(2)}) copy-start(f32[12,32]{1,0:T(8,128)S(1)} %get-tuple-element.63) | copy-start | bytes 4612
  1418.7 45.4 %copy-start.33 = (f32[12,32]{1,0:T(8,128)S(1)}, f32[12,32]{1,0:T(8,128)}, u32[]{:S(2)}) copy-start(f32[12,32]{1,0:T(8,128)} %param.20) | copy-start | bytes 4612
  1418.7 46.1 %copy-start.6 = (f32[256,512]{1,0:T(8,128)S(1)}, f32[256,512]{1,0:T(8,128)}, u32[]{:S(2)}) copy-start(f32[256,512]{1,0:T(8,128)} %param.19) | copy-start | bytes 1572868
  1418.7 46.1 %copy-start.10 = (f32[256,512]{1,0:T(8,128)S(1)}, f32[256,512]{1,0:T(8,128)}, u32[]{:S(2)}) copy-start(f32[256,512]{1,0:T(8,128)} %reduce-scatter.28.cloned.1.call-done) | copy-start | bytes 1572868
  (32 other events, 102.3 us)
Sparse Core Ops, SparseCore 0:
  17.2 63.0 all-gather.8
  82.5 40.1 all-gather.14
  124.8 31.7 all-gather.12
  158.6 33.0 all-gather.10
  193.7 74.2 all-gather.16
  270.1 72.8 all-gather.18
  345.3 97.8 reduce-scatter.11
  445.5 54.3 reduce-scatter.17
  502.2 189.2 reduce-scatter.21
  693.6 189.2 reduce-scatter.25
  885.2 144.5 reduce-scatter.13
  1033.9 61.7 reduce-scatter.19
  1098.6 9.9 reduce-scatter.29
  1113.1 103.9 reduce-scatter.23
  1221.6 103.0 reduce-scatter.27
  1329.0 84.6 reduce-scatter.15
where the time goes:
time: 1490 us; the launch traced here: 1480 us
  waiting for transfers between devices  1040 us (70%)
  matrix products  187 us (13%)
  blocking collectives  163 us (11%)
  other arithmetic  44.8 us (3%)
  local copies, waits for them, and re-layouts  28.9 us (2%)
  between operations  18.9 us (1%)
    reduce_scatter x1, waiting for transfers between devices, shards(): lax.psum_scatter(down_part, 'shard', scatter_dimension=1, tiled=True)  191 us
    reduce_scatter x1, waiting for transfers between devices, shards(): lax.psum_scatter(up_part, 'shard', scatter_dimension=1, tiled=True)  169 us
    reduce_scatter x1, waiting for transfers between devices, shards(): lax.psum_scatter(qkv_part, 'shard', scatter_dimension=1, tiled=True)  147 us
    reduce_scatter x1, waiting for transfers between devices, shards(): lax.psum_scatter(group_sums[3], 'dp', scatter_dimension=0, tiled=True)  106 us
    reduce_scatter x1, waiting for transfers between devices, shards(): lax.psum_scatter(group_sums[0], 'dp', scatter_dimension=0, tiled=True)  87.3 us
    unnamed x1, blocking collectives  65.1 us
    all_gather x1, waiting for transfers between devices, shards(): lax.all_gather(columns_full[3], 'dp', axis=0, tiled=True)  60.7 us
    reduce_scatter x1, waiting for transfers between devices, shards(): lax.psum_scatter(group_sums[1], 'dp', scatter_dimension=0, tiled=True)  53.7 us
  transfers between devices with their start and end apart: 16, of which 15 were waited for; matrix products, arithmetic and copies ran while one was open for 16% of the time, Pallas kernels for 0%

commit v1 on v0

--- a/solution.py
+++ b/solution.py
@@ -147,8 +147,18 @@
     cosine_table, sine_table = rotary_tables(positions, ROT)
     query_bf = rotate(query_raw, cosine_table, sine_table).astype(jnp.bfloat16)
     key_bf = rotate(key_raw, cosine_table, sine_table).astype(jnp.bfloat16).reshape(local_rows, D)
-    key_piece = lax.all_gather(key_bf, "shard", axis=0, tiled=True)
-    value_piece = lax.all_gather(value_bf, "shard", axis=0, tiled=True)
+
+    def _switch_links(body, axis_id, tile_in):
+        long_array = jnp.split(
+            lax.all_gather(
+                jnp.concatenate([tile_in, body], axis=1), axis_name=axis_id, axis=0, tiled=True
+            ),
+            [tile_in.shape[1]],
+            axis=1,
+        )
+        return long_array
+
+    key_piece, value_piece = _switch_links(value_bf, "shard", key_bf)
     piece_rows = key_piece.shape[0]
     key_heads = key_piece.reshape(piece_rows, head_count, HD)
     value_heads = value_piece.reshape(piece_rows, head_count, HD)

time: 1490 us -> 1550 us (1.040)
  waiting for transfers between devices: 1040 us -> 1060 us
  local copies, waits for them, and re-layouts: 28.9 us -> 45.3 us
    reduce_scatter x1, waiting for transfers between devices: 42.1 us -> 106 us  [shards(): lax.psum_scatter(group_sums[2], 'dp', scatter_dimension=0, tiled=True)]
    reduce_scatter x1, waiting for transfers between devices: 106 us -> 42.1 us  [shards(): lax.psum_scatter(group_sums[3], 'dp', scatter_dimension=0, tiled=True)]
    all_gather x2 -> x3, waiting for transfers between devices: 45.6 us -> 98.9 us  [the longest x1 42 us: _switch_links(): lax.all_gather(jnp.concatenate([tile_in, body], axis=1), axis_name=axis_i...]
    all_gather x1, waiting for transfers between devices: 60.7 us -> 25.2 us  [shards(): lax.all_gather(columns_full[3], 'dp', axis=0, tiled=True)]
    reduce_scatter x1, waiting for transfers between devices: 191 us -> 168 us  [shards(): lax.psum_scatter(down_part, 'shard', scatter_dimension=1, tiled=True)]
    reduce_scatter x1, waiting for transfers between devices: 169 us -> 191 us  [shards(): lax.psum_scatter(up_part, 'shard', scatter_dimension=1, tiled=True)]
    dot_general x1 -> x2, matrix products: 17.5 us -> 33.6 us  [shards(): jnp.einsum('qhd,khd->hqk', query_bf, key_heads, preferred_element_type=jn...]
  transfers between devices with their start and end apart: 16 -> 17, of which waited for: 15 -> 15; matrix products, arithmetic and copies ran while one was open for 16% -> 17% of each run, Pallas kernels for 0% -> 0%
where the time goes in v1:
time: 1550 us; the launch traced here: 1540 us
  waiting for transfers between devices  1060 us (68%)
  matrix products  202 us (13%)
  blocking collectives  163 us (11%)
  other arithmetic  46.5 us (3%)
  local copies, waits for them, and re-layouts  45.3 us (3%)
  between operations  19.2 us (1%)
    reduce_scatter x1, waiting for transfers between devices, shards(): lax.psum_scatter(up_part, 'shard', scatter_dimension=1, tiled=True)  191 us
    reduce_scatter x1, waiting for transfers between devices, shards(): lax.psum_scatter(down_part, 'shard', scatter_dimension=1, tiled=True)  168 us
    reduce_scatter x1, waiting for transfers between devices, shards(): lax.psum_scatter(qkv_part, 'shard', scatter_dimension=1, tiled=True)  147 us
    reduce_scatter x1, waiting for transfers between devices, shards(): lax.psum_scatter(group_sums[2], 'dp', scatter_dimension=0, tiled=True)  106 us
    reduce_scatter x1, waiting for transfers between devices, shards(): lax.psum_scatter(group_sums[0], 'dp', scatter_dimension=0, tiled=True)  87.3 us
    unnamed x1, blocking collectives  65.1 us
    reduce_scatter x1, waiting for transfers between devices, shards(): lax.psum_scatter(jnp.concatenate([key_terms, value_terms], axis=1), 'shar...  62.8 us
    reduce_scatter x1, waiting for transfers between devices, shards(): lax.psum_scatter(group_sums[1], 'dp', scatter_dimension=0, tiled=True)  53.9 us
  transfers between devices with their start and end apart: 17, of which 15 were waited for; matrix products, arithmetic and copies ran while one was open for 17% of the time, Pallas kernels for 0%

profile of v1, /device:TPU:0, one launch (start us, length us, event | category | flops | bytes accessed | tf_op | source)
XLA Modules:
  0.0 1538.2 jit_solution(15526165931220188069)
XLA Ops:
  8.4 8.6 all_gather.41
  27.6 22.3 %all-gather.1 = bf16[16,64,12]{1,2,0:T(8,128)(2,1)S(1)} all-gather(bf16[1,64,12]{1,2,0:T(8,128)(2,1)S(1)} %reshape.343), channel_id=1, replica_groups=mesh['dp'=16,'shard'=2] {'dp'}, dimensions={0}, use_global_device_ids=true | all-gather | bytes 26112 | tf_op jit(solution)/shard_map/all_gather | solution.py:129
  51.3 29.0 %all-gather.10.cloned.1.call-done = bf16[1024,3072]{1,0:T(8,128)(2,1)} async-done(((bf16[64,3072]{1,0:T(8,128)(2,1)}), bf16[1024,3072]{1,0:T(8,128)(2,1)}) %all-gather.10.cloned.1.call-update) | async-done | bytes 6291472 | tf_op jit(solution)/shard_map/all_gather | solution.py:125
  103.7 9.4 all_gather.46
  130.4 26.3 %all-gather.22.cloned.1.call-done = bf16[1024,1024]{1,0:T(8,128)(2,1)} async-done(((bf16[512,1024]{1,0:T(8,128)(2,1)}), bf16[1024,1024]{1,0:T(8,128)(2,1)}) %all-gather.22.cloned.1.call-update) | async-done | bytes 2097168 | tf_op jit(solution)/shard_map/all_gather | solution.py:212
  160.7 30.5 %all-gather.20.cloned.1.call-done = bf16[1024,1024]{0,1:T(8,128)(2,1)} async-done(((bf16[512,1024]{0,1:T(8,128)(2,1)}), bf16[1024,1024]{0,1:T(8,128)(2,1)}) %all-gather.20.cloned.1.call-update) | async-done | bytes 2097168 | tf_op jit(solution)/shard_map/all_gather | solution.py:211
  191.2 16.7 %fusion.62 = f32[16,512,1024]{2,1,0:T(8,128)} fusion(bf16[1024,16,64]{0,2,1:T(8,128)(2,1)} %bitcast.171, bf16[512,16,48]{0,2,1:T(8,128)(2,1)S(1)} %slice.266, bf16[512,16,8]{0,2,1:T(8,128)(2,1)S(1)} %copy-done.14, bf16[512,16,8]{0,2,1:T(8,128)(2,1)S(1)} %get-tuple-element.75), kind=kOutput, calls=%fused_computation.163 | convolution fusion | flops 1076887552 | bytes 36700160 | tf_op jit(solution)/shard_map/qhd,khd->hqk/dot_general | solution.py:221
  207.9 42.0 %all-gather.12.cloned.1.call-done = bf16[1024,2048]{1,0:T(8,128)(2,1)} async-done(((bf16[512,2048]{1,0:T(8,128)(2,1)}), bf16[1024,2048]{1,0:T(8,128)(2,1)}) %all-gather.12.cloned.1.call-update) | async-done | bytes 4194320 | tf_op jit(solution)/shard_map/all_gather | solution.py:153
  260.4 16.9 %fusion = (f32[16,512]{1,0:T(8,128)S(1)}, f32[16,512,1024]{2,1,0:T(8,128)}) fusion(pred[512,1024]{1,0:T(8,128)(4,1)} %fusion.19, bf16[1024,16,64]{0,2,1:T(8,128)(2,1)} %bitcast.184, bf16[512,16,48]{0,2,1:T(8,128)(2,1)S(1)} %slice.266, bf16[512,16,8]{0,2,1:T(8,128)(2,1)S(1)} %copy-done.14, bf16[512,16,8]{0,2,1:T(8,128)(2,1)S(1)} %get-tuple-element.75), kind=kOutput, calls=%fused_computation.3 | convolution fusion | flops 1102045184 | bytes 37257216 | tf_op jit(solution)/shard_map/qhd,khd->hqk/dot_general | solution.py:170
  277.3 16.6 %multiply_reduce_fusion.4 = (f32[512,16]{0,1:T(8,128)S(1)}, bf16[512,16,64]{0,2,1:T(8,128)(2,1)}) fusion(bf16[512,1024]{0,1:T(8,128)(2,1)} %copy.84, f32[512,16]{0,1:T(8,128)S(1)} %bitcast.195, bf16[1024,16,64]{0,2,1:T(8,128)(2,1)} %bitcast.183, f32[16,512,1024]{2,1,0:T(8,128)} %get-tuple-element.115, pred[512,1024]{1,0:T(8,128)(4,1)} %fusion.19), kind=kOutput, calls=%fused_computation.35 | convolution fusion | flops 1101520896 | bytes 38338560 | tf_op jit(solution)/shard_map/hqk,khd->qhd/dot_general | solution.py:174
  293.9 22.6 %multiply_convert_fusion = bf16[16,512,1024]{2,1,0:T(8,128)(2,1)} fusion(f32[16,512,1024]{2,1,0:T(8,128)} %fusion.62, f32[16,512]{1,0:T(8,128)S(1)} %bitcast.217, f32[16,512]{1,0:T(8,128)S(1)} %log.7, pred[512,1024]{1,0:T(8,128)(4,1)} %fusion.19, bf16[512,16,64]{0,2,1:T(8,128)(2,1)} %bitcast.189, bf16[1024,16,64]{0,2,1:T(8,128)(2,1)S(1)} %bitcast.182), kind=kOutput, calls=%fused_computation | convolution fusion | flops 1132462080 | bytes 54067200 | tf_op jit(solution)/shard_map/qhd,khd->hqk/dot_general | solution.py:225
  316.5 9.1 fusion.61
  325.7 17.1 %fusion.5 = f32[16,64,1024]{2,1,0:T(8,128)} fusion(bf16[512,16,64]{0,2,1:T(8,128)(2,1)} %bitcast.190, f32[16,512,1024]{2,1,0:T(8,128)} %fusion.62, f32[16,512]{1,0:T(8,128)} %copy-done.32, pred[512,1024]{1,0:T(8,128)(4,1)} %fusion.19), kind=kOutput, calls=%fused_computation.7 | convolution fusion | flops 1107296256 | bytes 39354368 | tf_op jit(solution)/shard_map/hqk,qhd->khd/dot_general | solution.py:239
  356.0 9.9 multiply_convert_fusion.1
  376.2 25.2 %all-gather.18.cloned.1.call-done = bf16[4096,1024]{1,0:T(8,128)(2,1)} async-done(((bf16[256,1024]{1,0:T(8,128)(2,1)}), bf16[4096,1024]{1,0:T(8,128)(2,1)}) %all-gather.18.cloned.1.call-update) | async-done | bytes 8388624 | tf_op jit(solution)/shard_map/all_gather | solution.py:128
  401.4 10.7 fusion.68
  422.9 13.2 convolution_bitcast_fusion
  438.8 62.8 %reduce-scatter.12.cloned.1.call-done = f32[512,2048]{0,1:T(8,128)} async-done(((f32[1024,2048]{0,1:T(8,128)}), f32[512,2048]{0,1:T(8,128)}) %reduce-scatter.12.cloned.1.call-update) | async-done | bytes 4194320 | tf_op jit(solution)/shard_map/reduce_scatter | solution.py:245
  509.3 9.6 fusion.24
  519.8 38.5 %reduce-scatter.18.cloned.1.call-done = f32[1024,512]{1,0:T(8,128)} async-done(((f32[1024,1024]{1,0:T(8,128)}), f32[1024,512]{1,0:T(8,128)}) %reduce-scatter.18.cloned.1.call-update) | async-done | bytes 2097168 | tf_op jit(solution)/shard_map/reduce_scatter | solution.py:282
  558.6 8.5 fusion.25
  569.0 11.7 multiply_reduce_fusion
  581.8 167.8 %reduce-scatter.26.cloned.1.call-done = f32[4096,512]{1,0:T(8,128)} async-done(((f32[4096,1024]{1,0:T(8,128)}), f32[4096,512]{1,0:T(8,128)}) %reduce-scatter.26.cloned.1.call-update) | async-done | bytes 8388624 | tf_op jit(solution)/shard_map/reduce_scatter | solution.py:284
  749.7 191.5 %reduce-scatter.22.cloned.1.call-done = f32[1024,2048]{1,0:T(8,128)} async-done(((f32[1024,4096]{1,0:T(8,128)}), f32[1024,2048]{1,0:T(8,128)}) %reduce-scatter.22.cloned.1.call-update) | async-done | bytes 8388624 | tf_op jit(solution)/shard_map/reduce_scatter | solution.py:283
  941.3 146.7 %reduce-scatter.14.cloned.1.call-done = f32[1024,1536]{1,0:T(8,128)} async-done(((f32[1024,3072]{1,0:T(8,128)}), f32[1024,1536]{1,0:T(8,128)}) %reduce-scatter.14.cloned.1.call-update) | async-done | bytes 6291472 | tf_op jit(solution)/shard_map/reduce_scatter | solution.py:281
  1100.2 53.9 %reduce-scatter.20.cloned.1.call-done = f32[64,512]{1,0:T(8,128)} async-done(((f32[1024,512]{1,0:T(8,128)}), f32[64,512]{1,0:T(8,128)}) %reduce-scatter.20.cloned.1.call-update) | async-done | bytes 131088 | tf_op jit(solution)/shard_map/reduce_scatter | solution.py:289
  1155.6 11.1 reduce-scatter.30.cloned.1.call-done
  1166.8 65.1 %all-reduce = f32[12,16,1,32]{3,2,1,0:T(1,128)S(1)} all-reduce(f32[12,16,1,32]{3,2,1,0:T(1,128)} %bitcast.193), channel_id=12, replica_groups=mesh['dp'=16,'shard'=2] {'dp'}, use_global_device_ids=true, to_apply=%region_28.29.clone | all-reduce | flops 6144 | bytes 49152
  1233.1 42.1 %reduce-scatter.28.cloned.1.call-done = f32[256,512]{1,0:T(8,128)} async-done(((f32[4096,512]{1,0:T(8,128)}), f32[256,512]{1,0:T(8,128)}) %reduce-scatter.28.cloned.1.call-update) | async-done | bytes 524304 | tf_op jit(solution)/shard_map/reduce_scatter | solution.py:291
  1277.0 105.8 %reduce-scatter.24.cloned.1.call-done = f32[64,2048]{1,0:T(8,128)} async-done(((f32[1024,2048]{1,0:T(8,128)}), f32[64,2048]{1,0:T(8,128)}) %reduce-scatter.24.cloned.1.call-update) | async-done | bytes 524304 | tf_op jit(solution)/shard_map/reduce_scatter | solution.py:290
  1384.6 87.3 %reduce-scatter.16.cloned.1.call-done = f32[64,1536]{1,0:T(8,128)} async-done(((f32[1024,1536]{1,0:T(8,128)}), f32[64,1536]{1,0:T(8,128)}) %reduce-scatter.16.cloned.1.call-update) | async-done | bytes 393232 | tf_op jit(solution)/shard_map/reduce_scatter | solution.py:288
  1481.4 39.6 %psum.7 = f32[]{:T(128)} all-reduce(f32[]{:T(128)S(6)} %add.283), channel_id=1, replica_groups=mesh['dp'=16,'shard'=2] {'dp','shard'}, use_global_device_ids=true, to_apply=%region_34.35 | all-reduce | flops 1 | bytes 8 | tf_op jit(solution)/shard_map/psum | solution.py:306
  (242 shorter events, 150.8 us)
Async XLA Ops:
  7.2 42.8 %copy-start = (f32[512,1024]{1,0:T(8,128)S(1)}, f32[512,1024]{1,0:T(8,128)}, u32[]{:S(2)}) copy-start(f32[512,1024]{1,0:T(8,128)} %param.13) | copy-start | bytes 6291460
  7.2 73.1 %all-gather.10.cloned.1.call-start = ((), (), s32[]{:S(2)}) async-start(), calls=%async_computation.10 | async-start | bytes 6684672 | tf_op jit(solution)/shard_map/all_gather | solution.py:125
  17.1 106.8 %all-gather.14.cloned.1.call-start = ((), (), s32[]{:S(2)}) async-start(), calls=%async_computation.12 | async-start | bytes 2228224 | tf_op jit(solution)/shard_map/all_gather | solution.py:126
  23.1 133.6 %all-gather.22.cloned.1.call-start = ((), (), s32[]{:S(2)}) async-start(), calls=%async_computation.16 | async-start | bytes 3145728 | tf_op jit(solution)/shard_map/all_gather | solution.py:212
  51.3 34.8 %copy-start.36 = (f32[1,1024]{1,0:T(1,128)}, f32[1,1024]{1,0:T(1,128)S(1)}, u32[]{:S(2)}) copy-start(f32[1,1024]{1,0:T(1,128)S(1)} %get-tuple-element.102) | copy-start | bytes 12292
  51.3 34.8 %copy-start.42 = (f32[1,1024]{1,0:T(1,128)}, f32[1,1024]{1,0:T(1,128)S(1)}, u32[]{:S(2)}) copy-start(f32[1,1024]{1,0:T(1,128)S(1)} %get-tuple-element.101) | copy-start | bytes 12292
  88.4 102.8 %all-gather.20.cloned.1.call-start = ((), (), s32[]{:S(2)}) async-start(), calls=%async_computation.15 | async-start | bytes 3145728 | tf_op jit(solution)/shard_map/all_gather | solution.py:211
  99.4 150.5 %all-gather.12.cloned.1.call-start = ((), (), s32[]{:S(2)}) async-start(), calls=%async_computation.11 | async-start | bytes 6291456 | tf_op jit(solution)/shard_map/all_gather | solution.py:153
  102.6 252.8 %all-gather.16.cloned.1.call-start = ((), (), s32[]{:S(2)}) async-start(), calls=%async_computation.13 | async-start | bytes 8912896 | tf_op jit(solution)/shard_map/all_gather | solution.py:127
  103.6 19.4 %copy-start.4 = (f32[512,1024]{1,0:T(8,128)S(1)}, f32[512,1024]{1,0:T(8,128)}, u32[]{:S(2)}) copy-start(f32[512,1024]{1,0:T(8,128)} %param.14) | copy-start | bytes 6291460
  113.1 288.3 %all-gather.18.cloned.1.call-start = ((), (), s32[]{:S(2)}) async-start(), calls=%async_computation.14 | async-start | bytes 8912896 | tf_op jit(solution)/shard_map/all_gather | solution.py:128
  121.6 380.0 %reduce-scatter.12.cloned.1.call-start = ((), (), s32[]{:S(2)}) async-start(), calls=%async_computation.17 | async-start | bytes 12582912 | tf_op jit(solution)/shard_map/reduce_scatter | solution.py:245
  130.3 60.9 %copy-start.14 = (bf16[512,16,8]{0,2,1:T(8,128)(2,1)S(1)}, bf16[512,16,8]{0,2,1:T(8,128)(2,1)}, u32[]{:S(2)}) copy-start(bf16[512,16,8]{0,2,1:T(8,128)(2,1)} %get-tuple-element.76) | copy-start | bytes 393220
  277.3 16.6 %copy-start.32 = (f32[16,512]{1,0:T(8,128)}, f32[16,512]{1,0:T(8,128)S(1)}, u32[]{:S(2)}) copy-start(f32[16,512]{1,0:T(8,128)S(1)} %log.7) | copy-start | bytes 98308
  293.9 22.6 %copy-start.15 = (bf16[512,16,8]{0,2,1:T(8,128)(2,1)S(1)}, bf16[512,16,8]{0,2,1:T(8,128)(2,1)}, u32[]{:S(2)}) copy-start(bf16[512,16,8]{0,2,1:T(8,128)(2,1)} %get-tuple-element.76) | copy-start | bytes 393220
  349.6 208.7 %reduce-scatter.18.cloned.1.call-start = ((), (), s32[]{:S(2)}) async-start(), calls=%async_computation.20 | async-start | bytes 6291456 | tf_op jit(solution)/shard_map/reduce_scatter | solution.py:282
  354.4 395.3 %reduce-scatter.26.cloned.1.call-start = ((), (), s32[]{:S(2)}) async-start(), calls=%async_computation.24 | async-start | bytes 25165824 | tf_op jit(solution)/shard_map/reduce_scatter | solution.py:284
  376.1 565.1 %reduce-scatter.22.cloned.1.call-start = ((), (), s32[]{:S(2)}) async-start(), calls=%async_computation.22 | async-start | bytes 25165824 | tf_op jit(solution)/shard_map/reduce_scatter | solution.py:283
  422.6 665.3 %reduce-scatter.14.cloned.1.call-start = ((), (), s32[]{:S(2)}) async-start(), calls=%async_computation.18 | async-start | bytes 18874368 | tf_op jit(solution)/shard_map/reduce_scatter | solution.py:281
  518.9 635.2 %reduce-scatter.20.cloned.1.call-start = ((), (), s32[]{:S(2)}) async-start(), calls=%async_computation.21 | async-start | bytes 2228224 | tf_op jit(solution)/shard_map/reduce_scatter | solution.py:289
  558.3 608.4 %reduce-scatter.30.cloned.1.call-start = ((), (), s32[]{:S(2)}) async-start(), calls=%async_computation.26 | async-start | bytes 294912 | tf_op jit(solution)/shard_map/reduce_scatter | solution.py:285
  581.8 693.4 %reduce-scatter.28.cloned.1.call-start = ((), (), s32[]{:S(2)}) async-start(), calls=%async_computation.25 | async-start | bytes 8912896 | tf_op jit(solution)/shard_map/reduce_scatter | solution.py:291
  749.7 633.1 %reduce-scatter.24.cloned.1.call-start = ((), (), s32[]{:S(2)}) async-start(), calls=%async_computation.23 | async-start | bytes 8912896 | tf_op jit(solution)/shard_map/reduce_scatter | solution.py:290
  941.2 530.7 %reduce-scatter.16.cloned.1.call-start = ((), (), s32[]{:S(2)}) async-start(), calls=%async_computation.19 | async-start | bytes 6684672 | tf_op jit(solution)/shard_map/reduce_scatter | solution.py:288
  1233.1 288.6 %copy-start.35 = (f32[12,32]{1,0:T(8,128)}, f32[12,32]{1,0:T(8,128)S(1)}, u32[]{:S(2)}) copy-start(f32[12,32]{1,0:T(8,128)S(1)} %get-tuple-element.63) | copy-start | bytes 4612
  1476.9 44.9 %copy-start.34 = (f32[12,32]{1,0:T(8,128)S(1)}, f32[12,32]{1,0:T(8,128)}, u32[]{:S(2)}) copy-start(f32[12,32]{1,0:T(8,128)} %param.20) | copy-start | bytes 4612
  1476.9 46.1 %copy-start.24 = (f32[64,512]{1,0:T(8,128)S(1)}, f32[64,512]{1,0:T(8,128)}, u32[]{:S(2)}) copy-start(f32[64,512]{1,0:T(8,128)} %param.17) | copy-start | bytes 393220
  1476.9 46.1 %copy-start.25 = (f32[64,512]{1,0:T(8,128)S(1)}, f32[64,512]{1,0:T(8,128)}, u32[]{:S(2)}) copy-start(f32[64,512]{1,0:T(8,128)} %reduce-scatter.20.cloned.1.call-done) | copy-start | bytes 393220
  1476.9 46.1 %copy-start.26 = (f32[2,64,512]{2,1,0:T(8,128)S(1)}, f32[2,64,512]{2,1,0:T(8,128)}, u32[]{:S(2)}) copy-start(f32[2,64,512]{2,1,0:T(8,128)} %param.22) | copy-start | bytes 786436
  1476.9 47.6 %copy-start.12 = (f32[64,1536]{1,0:T(8,128)S(1)}, f32[64,1536]{1,0:T(8,128)}, u32[]{:S(2)}) copy-start(f32[64,1536]{1,0:T(8,128)} %param.16) | copy-start | bytes 1179652
  1476.9 47.6 %copy-start.13 = (f32[64,1536]{1,0:T(8,128)S(1)}, f32[64,1536]{1,0:T(8,128)}, u32[]{:S(2)}) copy-start(f32[64,1536]{1,0:T(8,128)} %reduce-scatter.16.cloned.1.call-done) | copy-start | bytes 1179652
  1481.4 43.1 %copy-start.23 = (f32[2,64,1536]{2,1,0:T(8,128)S(1)}, f32[2,64,1536]{2,1,0:T(8,128)}, u32[]{:S(2)}) copy-start(f32[2,64,1536]{2,1,0:T(8,128)} %param.21) | copy-start | bytes 2359300
  (35 other events, 130.6 us)
Sparse Core Ops, SparseCore 0:
  17.2 63.0 all-gather.9
  82.5 40.2 all-gather.13
  124.9 31.7 all-gather.21
  158.1 33.0 all-gather.19
  193.2 56.7 all-gather.11
  252.0 74.2 all-gather.15
  328.4 72.8 all-gather.17
  403.6 97.8 reduce-scatter.11
  503.9 54.3 reduce-scatter.17
  560.4 189.1 reduce-scatter.25
  752.0 189.1 reduce-scatter.21
  943.4 144.5 reduce-scatter.13
  1092.2 61.7 reduce-scatter.19
  1156.7 9.9 reduce-scatter.29
  1171.2 103.9 reduce-scatter.27
  1279.7 103.0 reduce-scatter.23
  1387.2 84.7 reduce-scatter.15
